TPU v7x, 32 devices: a whole 2x2x4 slice. The times are simulated.
32 devices in a mesh: parts: 2 (over y), bank: 8 (over z, x), batch: 2 (over core).
Axes of the slice: x: 2, y: 2, z: 4, core: 2. Of those that a mesh axis runs over, the one named last changes fastest.
Arguments:
- bank: bfloat16 [32768, 256], P(('parts', 'bank')), parts along dimension 0, may hold values from -1 to 1
- queries: bfloat16 [4096, 256], P(('parts', 'batch')), parts along dimension 0, may hold values from -8 to 8
- keys: bfloat16 [4096, 256], P(('parts', 'batch')), parts along dimension 0, may hold values from -0.375 to 0.375
- labels: int32 [4096], P(('parts', 'batch')), parts along dimension 0, may hold values from 0 to 2047, each once
- mask_tiles: int32 [32, 16], P('parts'), parts along dimension 0, may hold values from 0 to 127
Outputs:
- new_bank: bfloat16 [32768, 256], P(('parts', 'bank')), parts along dimension 0
- query_grad: float32 [4096, 256], P(('parts', 'batch')), parts along dimension 0
- loss: float32 [4096], P(('parts', 'batch')), parts along dimension 0
There are 2 independent parts, one for each index of `parts`. A program takes and returns all parts, laid end to end along the dimension named above; each array names one. Nothing has to cross between parts.
Inputs may be any that keep to these rules, and one draw needn't show every extreme that they name: `labels`: a permutation: each row of keys is the positive of exactly one query. `mask_tiles`: tile t holds bank rows t * 128 to t * 128 + 127; row b lists tiles excluded for queries b * 128 to b * 128 + 127; numbers may repeat.
All inputs are finite; a program needn't handle non-finite values.
Results may differ from a plain program's by a relative error of at most 0.0055.
Values may be sent and summed in bfloat16 or wider, within the bound.
A program may use at most 64 MiB of HBM per device.

v0:
```python
import jax
import jax.numpy as jnp
from jax import lax
from jax.sharding import PartitionSpec as P

TILE = 128
TAU = 0.12
NEG = -1e30
EPS = 1e-06


def masked_scores(rows_q, rows_k, mask_rows, first):
    s = jnp.einsum("qd,kd->qk", rows_q, rows_k, preferred_element_type=jnp.float32) / TAU
    nq, nk = s.shape
    ids = first + jnp.arange(nk // TILE, dtype=jnp.int32)
    hit = jnp.any(mask_rows[:, :, None] == ids[None, None, :], axis=1)
    live = jnp.broadcast_to(
        jnp.logical_not(hit)[:, None, :, None], (nq // TILE, TILE, nk // TILE, TILE)
    ).reshape(nq, nk)
    return (jnp.where(live, s, NEG), live)


def on_device(bank, queries, keys, labels, mask_tiles):
    qdev = queries.shape[0]
    bdev = bank.shape[0]
    total_bank = bdev * lax.axis_size("bank")
    total_query = qdev * lax.axis_size("batch")
    eta = 0.25 * total_bank / total_query
    mine = lax.axis_index("batch")
    first = lax.axis_index("bank") * (bdev // TILE)
    all_keys = lax.all_gather(keys, "batch", axis=0, tiled=True)
    key_rows = jnp.take(all_keys, labels, axis=0)
    pos = jnp.sum(queries.astype(jnp.float32) * key_rows.astype(jnp.float32), axis=1) / TAU
    own_mask = lax.dynamic_slice_in_dim(mask_tiles, mine * (qdev // TILE), qdev // TILE, 0)
    scores, live = masked_scores(queries, bank, own_mask, first)
    top = lax.pmax(jnp.max(scores, axis=1), "bank")
    part_sum = jnp.sum(jnp.where(live, jnp.exp(scores - top[:, None]), 0.0), axis=1)
    total = lax.psum(part_sum, "bank")
    high = jnp.maximum(top, pos)
    lse = high + jnp.log(total * jnp.exp(top - high) + jnp.exp(pos - high))
    loss = lse - pos
    probs = jnp.exp(scores - lse[:, None]).astype(jnp.bfloat16)
    neg_local = jnp.dot(probs, bank, preferred_element_type=jnp.float32)
    own_pull = jnp.einsum("qk,qd->kd", probs, queries, preferred_element_type=jnp.float32)
    neg = lax.psum(neg_local, "bank")
    query_grad = (neg + (jnp.exp(pos - lse) - 1.0)[:, None] * key_rows.astype(jnp.float32)) / TAU
    pull = lax.psum(own_pull.astype(jnp.bfloat16), "batch").astype(jnp.float32)
    fresh = bank.astype(jnp.float32) + eta * pull
    fresh = fresh * lax.rsqrt(jnp.mean(fresh * fresh, axis=1, keepdims=True) + EPS)
    return (fresh.astype(jnp.bfloat16), query_grad, loss)


def solution(mesh):
    return jax.shard_map(
        on_device,
        mesh=mesh,
        in_specs=(
            P(("parts", "bank"), None),
            P(("parts", "batch"), None),
            P(("parts", "batch"), None),
            P(("parts", "batch")),
            P("parts", None),
        ),
        out_specs=(P(("parts", "bank"), None), P(("parts", "batch"), None), P(("parts", "batch"))),
        check_vma=False,
    )
```

profile of v0, /device:TPU:0, one launch (start us, length us, event | category | flops | bytes accessed | tf_op | source)
XLA Modules:
  0.0 187.6 jit_solution(10827751201215872760)
XLA Ops:
  7.2 0.0 copy-start
  7.2 0.0 all-gather.2.cloned.1.call-start
  7.2 0.7 all-gather.2.cloned.1.call-update
  7.9 0.0 all-reduce.3.cloned.1.call-start
  8.0 0.0 copy-done
  8.0 0.1 compare_reduce_fusion
  8.1 0.6 broadcast_in_dim.31
  8.7 6.8 %fusion = (f32[1024]{0:T(1024)S(1)}, f32[1024,2048]{1,0:T(8,128)}) fusion(pred[128,8,16,128]{3,2,1,0:T(8,128)(4,1)S(1)} %bitcast.17, bf16[1024,256]{1,0:T(8,128)(2,1)} %param.6, bf16[2048,256]{1,0:T(8,128)(2,1)} %param.5), kind=kOutput, calls=%fused_computation.4 | convolution fusion | flops 1080032256 | bytes 12062720 | tf_op jit(solution)/shard_map/qd,kd->qk/dot_general | solution.py:13
  15.5 23.1 %pmax.7 = f32[1024]{0:T(1024)S(1)} all-reduce(f32[1024]{0:T(1024)S(1)} %get-tuple-element.5), channel_id=1, replica_groups=mesh['parts'=2,'bank'=8,'batch'=2] {'bank'}, use_global_device_ids=true, to_apply=%region_2.3 | all-reduce | flops 1024 | bytes 8192 | tf_op jit(solution)/shard_map/pmax | solution.py:36
  38.6 5.3 %select_reduce_fusion = f32[1024]{0:T(1024)S(1)} fusion(pred[128,8,16,128]{3,2,1,0:T(8,128)(4,1)S(1)} %bitcast.18, f32[1024,2048]{1,0:T(8,128)} %get-tuple-element.6, f32[1024]{0:T(1024)S(1)} %pmax.7), kind=kLoop, calls=%fused_computation.2 | loop fusion | flops 10484736 | bytes 10493952 | tf_op jit(solution)/shard_map/reduce_sum | solution.py:37
  43.9 0.0 copy-start.3
  43.9 17.3 %psum.21 = f32[1024]{0:T(1024)S(1)} all-reduce(f32[1024]{0:T(1024)S(1)} %select_reduce_fusion), channel_id=1, replica_groups=mesh['parts'=2,'bank'=8,'batch'=2] {'bank'}, use_global_device_ids=true, to_apply=%region_5.6 | all-reduce | flops 1024 | bytes 8192 | tf_op jit(solution)/shard_map/psum | solution.py:38
  61.2 0.0 copy-done.4
  61.2 0.0 all-gather.2.cloned.1.call-done
  61.2 4.8 %gather_fusion = bf16[1024,256]{1,0:T(8,128)(2,1)S(1)} fusion(bf16[2048,256]{1,0:T(8,128)(2,1)} %all-gather.2.cloned.1.call-done, s32[1024]{0:T(1024)S(1)} %fusion.6), kind=kCustom, calls=%fused_computation | custom fusion | bytes 1052672 | tf_op jit(solution)/shard_map/jit(_take)/gather | solution.py:32
  66.1 0.0 copy-done.3
  66.1 0.5 fusion.1
  66.6 0.6 multiply_subtract_fusion
  67.2 5.5 %exponential_convert_fusion = bf16[1024,2048]{1,0:T(8,128)(2,1)S(1)} fusion(f32[1024,2048]{1,0:T(8,128)} %get-tuple-element.6, pred[128,8,16,128]{3,2,1,0:T(8,128)(4,1)S(1)} %bitcast.19, f32[1024]{0:T(1024)S(1)} %get-tuple-element.4), kind=kLoop, calls=%fused_computation.1 | loop fusion | flops 8388608 | bytes 14684160 | tf_op jit(solution)/shard_map/convert_element_type | solution.py:42
  72.7 0.0 copy-start.2
  72.7 1.9 %copy-done.2 = bf16[1024,2048]{1,0:T(8,128)(2,1)} copy-done((bf16[1024,2048]{1,0:T(8,128)(2,1)}, bf16[1024,2048]{1,0:T(8,128)(2,1)S(1)}, u32[]{:S(2)}) %copy-start.2) | copy-done | bytes 4194328
  74.6 2.4 %convolution_convert_fusion = bf16[2048,256]{1,0:T(8,128)(2,1)} fusion(bf16[1024,2048]{1,0:T(8,128)(2,1)S(1)} %exponential_convert_fusion, bf16[1024,256]{1,0:T(8,128)(2,1)S(1)} %copy-done.3), kind=kOutput, calls=%fused_computation.5 | convolution fusion | flops 1074266112 | bytes 5767168 | tf_op jit(solution)/shard_map/qk,qd->kd/dot_general | solution.py:44
  77.0 0.0 all-reduce.3.cloned.1.call-update
  77.0 0.0 all-reduce.5.cloned.1.call-start
  77.0 0.0 copy-done.1
  77.0 4.5 %fusion.7 = f32[1024,256]{1,0:T(8,128)} fusion(bf16[1024,2048]{1,0:T(8,128)(2,1)} %copy-done.2, bf16[2048,256]{1,0:T(8,128)(2,1)S(1)} %copy-done.1), kind=kOutput, calls=%fused_computation.28 | convolution fusion | flops 1073741824 | bytes 6291456 | tf_op jit(solution)/shard_map/dot_general | solution.py:43
  81.5 0.0 all-reduce.5.cloned.1.call-update
  81.6 13.9 %all-reduce.3.cloned.1.call-done = bf16[2048,256]{1,0:T(8,128)(2,1)} async-done(((bf16[2048,256]{1,0:T(8,128)(2,1)}), bf16[2048,256]{1,0:T(8,128)(2,1)}) %all-reduce.3.cloned.1.call-update) | async-done | bytes 1048592 | tf_op jit(solution)/shard_map/psum | solution.py:47
  95.5 1.7 multiply_reduce_fusion
  97.2 2.6 %multiply_convert_fusion = bf16[2048,256]{1,0:T(8,128)(2,1)} fusion(bf16[2048,256]{1,0:T(8,128)(2,1)} %all-reduce.3.cloned.1.call-done, bf16[2048,256]{1,0:T(8,128)(2,1)S(1)} %copy-done.1, f32[2048]{0:T(1024)S(1)} %add_rsqrt_fusion), kind=kLoop, calls=%fused_computation.6 | loop fusion | flops 3145728 | bytes 3153920 | tf_op jit(solution)/shard_map/convert_element_type | solution.py:50
  99.8 78.7 %all-reduce.5.cloned.1.call-done = f32[1024,256]{1,0:T(8,128)} async-done(((f32[1024,256]{1,0:T(8,128)}), f32[1024,256]{1,0:T(8,128)}) %all-reduce.5.cloned.1.call-update) | async-done | bytes 1048592 | tf_op jit(solution)/shard_map/psum | solution.py:45
  178.6 2.5 %fusion.3 = f32[1024,256]{1,0:T(8,128)} fusion(f32[1024,256]{1,0:T(8,128)} %all-reduce.5.cloned.1.call-done, f32[1024]{0:T(1024)S(1)} %exponential_add_fusion, bf16[1024,256]{1,0:T(8,128)(2,1)S(1)} %gather_fusion, pred[1024]{0:T(1024)(128)(4,1)S(1)} %compare_and_fusion), kind=kLoop, calls=%fused_computation.13 | loop fusion | flops 1310720 | bytes 2626560 | tf_op jit(solution)/shard_map/div | solution.py:46
  (9 shorter events, 0.1 us)
Async XLA Ops:
  7.2 0.8 copy-start
  7.2 54.1 %all-gather.2.cloned.1.call-start = ((), (), s32[]{:S(2)}) async-start(), calls=%async_computation | async-start | bytes 1572864 | tf_op jit(solution)/shard_map/all_gather | solution.py:31
  7.9 87.6 %all-reduce.3.cloned.1.call-start = ((), (), s32[]{:S(2)}) async-start(), calls=%async_computation.1 | async-start | bytes 2097152 | tf_op jit(solution)/shard_map/psum | solution.py:47
  38.6 22.6 %copy-start.4 = (s32[1024]{0:T(1024)S(1)}, s32[1024]{0:T(1024)}, u32[]{:S(2)}) copy-start(s32[1024]{0:T(1024)} %param.8) | copy-start | bytes 12292
  43.9 22.2 %copy-start.3 = (bf16[1024,256]{1,0:T(8,128)(2,1)S(1)}, bf16[1024,256]{1,0:T(8,128)(2,1)}, u32[]{:S(2)}) copy-start(bf16[1024,256]{1,0:T(8,128)(2,1)} %param.6) | copy-start | bytes 1572868
  72.7 1.9 %copy-start.2 = (bf16[1024,2048]{1,0:T(8,128)(2,1)}, bf16[1024,2048]{1,0:T(8,128)(2,1)S(1)}, u32[]{:S(2)}) copy-start(bf16[1024,2048]{1,0:T(8,128)(2,1)S(1)} %exponential_convert_fusion) | copy-start | bytes 12582916
  74.6 2.4 %copy-start.1 = (bf16[2048,256]{1,0:T(8,128)(2,1)S(1)}, bf16[2048,256]{1,0:T(8,128)(2,1)}, u32[]{:S(2)}) copy-start(bf16[2048,256]{1,0:T(8,128)(2,1)} %param.5) | copy-start | bytes 3145732
  77.0 101.6 %all-reduce.5.cloned.1.call-start = ((), (), s32[]{:S(2)}) async-start(), calls=%async_computation.2 | async-start | bytes 2097152 | tf_op jit(solution)/shard_map/psum | solution.py:45
Sparse Core Ops, SparseCore 0:
  9.6 11.7 all-gather.1
  77.1 18.3 all-reduce.2
  99.4 79.1 all-reduce.4
where the time goes:
time: 188 us
  waiting for transfers between devices  93.4 us (50%)
  blocking collectives  40.3 us (21%)
  other arithmetic  18.9 us (10%)
  between operations  13.9 us (7%)
  matrix products  13.6 us (7%)
  local copies, waits for them, and re-layouts  7.38 us (4%)
    psum x1, waiting for transfers between devices, on_device(): neg = lax.psum(neg_local, 'bank')  78.7 us
    pmax x1, blocking collectives, on_device(): top = lax.pmax(jnp.max(scores, axis=1), 'bank')  23.1 us
    psum x1, blocking collectives, on_device(): total = lax.psum(part_sum, 'bank')  17.3 us
    psum x1, waiting for transfers between devices, on_device(): pull = lax.psum(own_pull.astype(jnp.bfloat16), 'batch').astype(jnp.float32)  13.9 us
    dot_general x1, matrix products, masked_scores(): jnp.einsum('qd,kd->qk', rows_q, rows_k, preferred_element_type=jnp.float32)  6.76 us
    convert_element_type x1, other arithmetic, on_device(): probs = jnp.exp(scores - lse[:, None]).astype(jnp.bfloat16)  5.45 us
    reduce_sum x1, other arithmetic, on_device(): jnp.sum(jnp.where(live, jnp.exp(scores - top[:, None]), 0.0), axis=1)  5.32 us
    gather x1, local copies, waits for them, and re-layouts, on_device(): key_rows = jnp.take(all_keys, labels, axis=0)  4.82 us
  transfers between devices with their start and end apart: 3, of which 2 were waited for; matrix products, arithmetic and copies ran while one was open for 12% of the time, Pallas kernels for 0%

commit v1 on v0

--- a/solution.py
+++ b/solution.py
@@ -44,7 +44,9 @@
     own_pull = jnp.einsum("qk,qd->kd", probs, queries, preferred_element_type=jnp.float32)
     neg = lax.psum(neg_local, "bank")
     query_grad = (neg + (jnp.exp(pos - lse) - 1.0)[:, None] * key_rows.astype(jnp.float32)) / TAU
-    pull = lax.psum(own_pull.astype(jnp.bfloat16), "batch").astype(jnp.float32)
+    pull = jnp.sum(lax.all_gather(own_pull.astype(jnp.bfloat16), "batch"), axis=0).astype(
+        jnp.float32
+    )
     fresh = bank.astype(jnp.float32) + eta * pull
     fresh = fresh * lax.rsqrt(jnp.mean(fresh * fresh, axis=1, keepdims=True) + EPS)
     return (fresh.astype(jnp.bfloat16), query_grad, loss)

time: 188 us -> 178 us (0.947)
  waiting for transfers between devices: 93.4 us -> 82.7 us
    psum x1 -> x0, waiting for transfers between devices: 13.9 us -> none  [on_device(): pull = lax.psum(own_pull.astype(jnp.bfloat16), 'batch').astype(jnp.float32)]
    all_gather x0 -> x1, waiting for transfers between devices: none -> 9.87 us  [on_device(): lax.all_gather(own_pull.astype(jnp.bfloat16), 'batch')]
    psum x1, waiting for transfers between devices: 78.7 us -> 72.1 us  [on_device(): neg = lax.psum(neg_local, 'bank')]
    reduce_sum x0 -> x1, other arithmetic: none -> 2.64 us  [on_device(): jnp.sum(lax.all_gather(own_pull.astype(jnp.bfloat16), 'batch'), axis=0)]
    dot_general x1, matrix products: 4.47 us -> 2.22 us  [on_device(): neg_local = jnp.dot(probs, bank, preferred_element_type=jnp.float32)]
    dot_general x1, matrix products: 2.37 us -> 4.51 us  [on_device(): jnp.einsum('qk,qd->kd', probs, queries, preferred_element_type=jnp.float32)]
  transfers between devices with their start and end apart: 3 -> 3, of which waited for: 2 -> 2; matrix products, arithmetic and copies ran while one was open for 12% -> 11% of each run, Pallas kernels for 0% -> 0%
where the time goes in v1:
time: 178 us; the launch traced here: 177 us
  waiting for transfers between devices  82.7 us (46%)
  blocking collectives  40.3 us (23%)
  other arithmetic  19.2 us (11%)
  between operations  13.9 us (8%)
  matrix products  13.5 us (8%)
  local copies, waits for them, and re-layouts  7.39 us (4%)
    psum x1, waiting for transfers between devices, on_device(): neg = lax.psum(neg_local, 'bank')  72.1 us
    pmax x1, blocking collectives, on_device(): top = lax.pmax(jnp.max(scores, axis=1), 'bank')  23.1 us
    psum x1, blocking collectives, on_device(): total = lax.psum(part_sum, 'bank')  17.3 us
    all_gather x1, waiting for transfers between devices, on_device(): lax.all_gather(own_pull.astype(jnp.bfloat16), 'batch')  9.87 us
    dot_general x1, matrix products, masked_scores(): jnp.einsum('qd,kd->qk', rows_q, rows_k, preferred_element_type=jnp.float32)  6.76 us
    convert_element_type x1, other arithmetic, on_device(): probs = jnp.exp(scores - lse[:, None]).astype(jnp.bfloat16)  5.54 us
    reduce_sum x1, other arithmetic, on_device(): jnp.sum(jnp.where(live, jnp.exp(scores - top[:, None]), 0.0), axis=1)  5.32 us
    gather x1, local copies, waits for them, and re-layouts, on_device(): key_rows = jnp.take(all_keys, labels, axis=0)  4.82 us
  transfers between devices with their start and end apart: 3, of which 2 were waited for; matrix products, arithmetic and copies ran while one was open for 11% of the time, Pallas kernels for 0%

profile of v1, /device:TPU:0, one launch (start us, length us, event | category | flops | bytes accessed | tf_op | source)
XLA Modules:
  0.0 177.3 jit_solution(5425298959721711608)
XLA Ops:
  7.2 0.0 copy-start
  7.2 0.0 all-gather.4.cloned.1.call-start
  7.2 0.7 all-gather.4.cloned.1.call-update
  7.9 0.0 all-reduce.2.cloned.1.call-start
  8.0 0.1 compare_reduce_fusion
  8.1 0.6 broadcast_in_dim.31
  8.7 6.8 %fusion = (f32[1024]{0:T(1024)S(1)}, f32[1024,2048]{1,0:T(8,128)}) fusion(pred[128,8,16,128]{3,2,1,0:T(8,128)(4,1)S(1)} %bitcast.18, bf16[1024,256]{1,0:T(8,128)(2,1)} %param.6, bf16[2048,256]{1,0:T(8,128)(2,1)} %param.5), kind=kOutput, calls=%fused_computation.4 | convolution fusion | flops 1080032256 | bytes 12062720 | tf_op jit(solution)/shard_map/qd,kd->qk/dot_general | solution.py:13
  15.5 23.1 %pmax.7 = f32[1024]{0:T(1024)S(1)} all-reduce(f32[1024]{0:T(1024)S(1)} %get-tuple-element.5), channel_id=1, replica_groups=mesh['parts'=2,'bank'=8,'batch'=2] {'bank'}, use_global_device_ids=true, to_apply=%region_2.3 | all-reduce | flops 1024 | bytes 8192 | tf_op jit(solution)/shard_map/pmax | solution.py:36
  38.6 5.3 %select_reduce_fusion = f32[1024]{0:T(1024)S(1)} fusion(pred[128,8,16,128]{3,2,1,0:T(8,128)(4,1)S(1)} %bitcast.19, f32[1024,2048]{1,0:T(8,128)} %get-tuple-element.6, f32[1024]{0:T(1024)S(1)} %pmax.7), kind=kLoop, calls=%fused_computation.2 | loop fusion | flops 10484736 | bytes 10493952 | tf_op jit(solution)/shard_map/reduce_sum | solution.py:37
  43.9 0.0 copy-start.4
  43.9 17.3 %psum.14 = f32[1024]{0:T(1024)S(1)} all-reduce(f32[1024]{0:T(1024)S(1)} %select_reduce_fusion), channel_id=1, replica_groups=mesh['parts'=2,'bank'=8,'batch'=2] {'bank'}, use_global_device_ids=true, to_apply=%region_5.6 | all-reduce | flops 1024 | bytes 8192 | tf_op jit(solution)/shard_map/psum | solution.py:38
  61.2 0.0 all-gather.4.cloned.1.call-done
  61.2 4.8 %gather_fusion = bf16[1024,256]{1,0:T(8,128)(2,1)S(1)} fusion(bf16[2048,256]{1,0:T(8,128)(2,1)} %all-gather.4.cloned.1.call-done, s32[1024]{0:T(1024)S(1)} %fusion.6), kind=kCustom, calls=%fused_computation | custom fusion | bytes 1052672 | tf_op jit(solution)/shard_map/jit(_take)/gather | solution.py:32
  66.1 0.0 copy-done.4
  66.1 0.5 fusion.1
  66.6 0.6 multiply_subtract_fusion
  67.2 5.5 %exponential_convert_fusion = bf16[1024,2048]{1,0:T(8,128)(2,1)S(1)} fusion(f32[1024,2048]{1,0:T(8,128)} %get-tuple-element.6, pred[128,8,16,128]{3,2,1,0:T(8,128)(4,1)S(1)} %bitcast.20, f32[1024]{0:T(1024)S(1)} %get-tuple-element.4), kind=kLoop, calls=%fused_computation.1 | loop fusion | flops 8388608 | bytes 14684160 | tf_op jit(solution)/shard_map/convert_element_type | solution.py:42
  72.8 0.0 copy-start.3
  72.8 1.9 %copy-done.3 = bf16[1024,2048]{1,0:T(8,128)(2,1)} copy-done((bf16[1024,2048]{1,0:T(8,128)(2,1)}, bf16[1024,2048]{1,0:T(8,128)(2,1)S(1)}, u32[]{:S(2)}) %copy-start.3) | copy-done | bytes 4194328
  74.7 0.0 copy-done.1
  74.7 2.2 %fusion.7 = f32[1024,256]{1,0:T(8,128)} fusion(bf16[1024,2048]{1,0:T(8,128)(2,1)S(1)} %exponential_convert_fusion, bf16[2048,256]{1,0:T(8,128)(2,1)S(1)} %copy-done.1), kind=kOutput, calls=%fused_computation.28 | convolution fusion | flops 1073741824 | bytes 6291456 | tf_op jit(solution)/shard_map/dot_general | solution.py:43
  76.9 0.0 all-reduce.2.cloned.1.call-update
  76.9 0.2 all-gather.6.cloned.1.call-start
  77.2 4.5 %convolution_convert_fusion = bf16[2048,256]{1,0:T(8,128)(2,1)} fusion(bf16[1024,2048]{1,0:T(8,128)(2,1)} %copy-done.3, bf16[1024,256]{1,0:T(8,128)(2,1)S(1)} %copy-done.4), kind=kOutput, calls=%fused_computation.5 | convolution fusion | flops 1074266112 | bytes 5767168 | tf_op jit(solution)/shard_map/qk,qd->kd/dot_general | solution.py:44
  81.7 0.0 all-gather.6.cloned.1.call-update
  81.7 72.1 %all-reduce.2.cloned.1.call-done = f32[1024,256]{1,0:T(8,128)} async-done(((f32[1024,256]{1,0:T(8,128)}), f32[1024,256]{1,0:T(8,128)}) %all-reduce.2.cloned.1.call-update) | async-done | bytes 1048592 | tf_op jit(solution)/shard_map/psum | solution.py:45
  153.8 2.5 %fusion.3 = f32[1024,256]{1,0:T(8,128)} fusion(f32[1024,256]{1,0:T(8,128)} %all-reduce.2.cloned.1.call-done, f32[1024]{0:T(1024)S(1)} %exponential_add_fusion, bf16[1024,256]{1,0:T(8,128)(2,1)S(1)} %gather_fusion, pred[1024]{0:T(1024)(128)(4,1)S(1)} %compare_and_fusion), kind=kLoop, calls=%fused_computation.13 | loop fusion | flops 1310720 | bytes 2626560 | tf_op jit(solution)/shard_map/div | solution.py:46
  156.4 9.9 %all-gather.6.cloned.1.call-done = bf16[4096,256]{1,0:T(8,128)(2,1)} async-done(((bf16[2048,256]{1,0:T(8,128)(2,1)}), bf16[4096,256]{1,0:T(8,128)(2,1)}) %all-gather.6.cloned.1.call-update) | async-done | bytes 2097168 | tf_op jit(solution)/shard_map/all_gather | solution.py:47
  166.2 2.6 %reduce_sum.41 = bf16[2048,256]{1,0:T(8,128)(2,1)S(1)} reduce(bf16[2,2048,256]{2,1,0:T(8,128)(2,1)} %bitcast.21, bf16[]{:T(256)} %constant.51.clone.1), dimensions={0}, to_apply=%region_6.7 | reduce | flops 524288 | bytes 3145730 | tf_op jit(solution)/shard_map/reduce_sum | solution.py:47
  168.9 0.0 copy-done.2
  168.9 0.5 multiply_reduce_fusion
  169.4 1.4 multiply_convert_fusion
  (12 shorter events, 0.1 us)
Async XLA Ops:
  7.2 0.8 copy-start
  7.2 54.1 %all-gather.4.cloned.1.call-start = ((), (), s32[]{:S(2)}) async-start(), calls=%async_computation | async-start | bytes 1572864 | tf_op jit(solution)/shard_map/all_gather | solution.py:31
  7.9 145.9 %all-reduce.2.cloned.1.call-start = ((), (), s32[]{:S(2)}) async-start(), calls=%async_computation.1 | async-start | bytes 2097152 | tf_op jit(solution)/shard_map/psum | solution.py:45
  38.6 22.6 %copy-start.5 = (s32[1024]{0:T(1024)S(1)}, s32[1024]{0:T(1024)}, u32[]{:S(2)}) copy-start(s32[1024]{0:T(1024)} %param.8) | copy-start | bytes 12292
  43.9 22.2 %copy-start.4 = (bf16[1024,256]{1,0:T(8,128)(2,1)S(1)}, bf16[1024,256]{1,0:T(8,128)(2,1)}, u32[]{:S(2)}) copy-start(bf16[1024,256]{1,0:T(8,128)(2,1)} %param.6) | copy-start | bytes 1572868
  67.2 7.5 %copy-start.1 = (bf16[2048,256]{1,0:T(8,128)(2,1)S(1)}, bf16[2048,256]{1,0:T(8,128)(2,1)}, u32[]{:S(2)}) copy-start(bf16[2048,256]{1,0:T(8,128)(2,1)} %param.5) | copy-start | bytes 3145732
  72.8 1.9 %copy-start.3 = (bf16[1024,2048]{1,0:T(8,128)(2,1)}, bf16[1024,2048]{1,0:T(8,128)(2,1)S(1)}, u32[]{:S(2)}) copy-start(bf16[1024,2048]{1,0:T(8,128)(2,1)S(1)} %exponential_convert_fusion) | copy-start | bytes 12582916
  76.9 89.3 %all-gather.6.cloned.1.call-start = ((), (), s32[]{:S(2)}) async-start(), calls=%async_computation.2 | async-start | bytes 3145728 | tf_op jit(solution)/shard_map/all_gather | solution.py:47
  81.7 87.2 %copy-start.2 = (bf16[2048,256]{1,0:T(8,128)(2,1)S(1)}, bf16[2048,256]{1,0:T(8,128)(2,1)}, u32[]{:S(2)}) copy-start(bf16[2048,256]{1,0:T(8,128)(2,1)} %param.5) | copy-start | bytes 3145732
Sparse Core Ops, SparseCore 0:
  9.6 11.7 all-gather.3
  77.1 76.7 all-reduce.1
  156.0 10.1 all-gather.5
